TPU v7x, 32 devices: a whole 2x2x4 slice. The times are simulated.
32 devices in a mesh: inb: 4 (over y, x), outb: 8 (over z, core).
Axes of the slice: x: 2, y: 2, z: 4, core: 2. Of those that a mesh axis runs over, the one named last changes fastest.
Arguments:
- site_cores: float32 [2, 4, 8192, 8192], P(None, None, 'inb', 'outb')
- left_env: float32 [512, 8192], P(None, 'outb')
- outcomes: int32 [2, 512], replicated, may hold values from 0 to 3
Outputs:
- env_out: float32 [512, 8192], P('inb', 'outb')
- probabilities: float32 [2, 4, 512], P(None, None, 'inb')
- log_scale: float32 [512], P('inb')
All inputs are finite; a program needn't handle non-finite values.
Results may differ from a plain program's by a relative error of at most 0.00014.
Values sent between devices are 32-bit elements; how exact they have to be, the bound alone decides.
A program may use at most 128 MiB of HBM per device.

v0:
```python
import jax
import jax.numpy as jnp
from jax import lax
from jax.sharding import PartitionSpec as P

epsilon = 1e-06


def on_device(site_cores, left_env, outcomes):
    inb_index = lax.axis_index("inb")
    inb_count = lax.axis_size("inb")
    samples_all = left_env.shape[0]
    block_rows = samples_all // inb_count
    width_out = site_cores.shape[3]
    bond_width = width_out * lax.axis_size("outb")
    outcome_count = site_cores.shape[1]
    levels = jnp.arange(outcome_count, dtype=jnp.int32)
    current = lax.dynamic_slice_in_dim(left_env, inb_index * block_rows, block_rows, 0)
    chosen_ids = lax.dynamic_slice_in_dim(outcomes, inb_index * block_rows, block_rows, 1)
    log_scale = jnp.zeros((chosen_ids.shape[1],), jnp.float32)
    prob_list = []
    for site_index in range(site_cores.shape[0]):
        sample_rows = lax.all_gather(current, "outb", axis=1, tiled=True)
        own_cols = lax.all_to_all(sample_rows, "inb", split_axis=1, concat_axis=0, tiled=True)
        partial_terms = jnp.einsum(
            "sc,pcd->psd", own_cols, site_cores[site_index], precision=lax.Precision.HIGHEST
        )
        candidates = lax.psum_scatter(partial_terms, "inb", scatter_dimension=1, tiled=True)
        squares = jnp.sum(candidates * candidates, axis=2)
        totals = lax.psum(squares, "outb")
        mean_squares = totals / bond_width + epsilon
        prob_list.append(mean_squares / jnp.sum(mean_squares, axis=0, keepdims=True))
        onehot = (chosen_ids[site_index][None, :] == levels[:, None]).astype(jnp.float32)
        chosen = jnp.sum(onehot[:, :, None] * candidates, axis=0)
        chosen_mean = jnp.sum(onehot * mean_squares, axis=0)
        inverse = lax.rsqrt(chosen_mean)
        log_scale = log_scale + 0.5 * jnp.log(chosen_mean)
        current = chosen * inverse[:, None]
    prob_stack = jnp.stack(prob_list)
    return (current, prob_stack, log_scale)


def solution(mesh):
    in_specs = (P(None, None, "inb", "outb"), P(None, "outb"), P())
    out_specs = (P("inb", "outb"), P(None, None, "inb"), P("inb"))
    return jax.shard_map(
        on_device, mesh=mesh, in_specs=in_specs, out_specs=out_specs, check_vma=False
    )
```

profile of v0, /device:TPU:0, one launch (start us, length us, event | category | flops | bytes accessed | tf_op | source)
XLA Modules:
  0.0 555.6 jit_solution(1600820002237552070)
XLA Ops:
  7.2 1.5 copy-done
  8.8 0.8 constant_dynamic-slice_fusion
  9.6 0.0 reduce-scatter.3.cloned.1.call-start
  9.7 50.1 %all-gather.3.cloned.1.call-done = f32[128,8192]{1,0:T(8,128)} async-done(((f32[128,1024]{1,0:T(8,128)}), f32[128,8192]{1,0:T(8,128)}) %all-gather.3.cloned.1.call-update) | async-done | bytes 4194320 | tf_op jit(solution)/shard_map/all_gather | solution.py:23
  59.8 2.5 copy.14
  62.3 51.7 %all_to_all.38 = f32[128,4,2048]{2,0,1:T(8,128)S(1)} all-to-all(f32[128,4,2048]{2,0,1:T(8,128)S(1)} %bitcast.46), channel_id=1, replica_groups=mesh['inb'=4,'outb'=8] {'inb'}, dimensions={1} | all-to-all | bytes 8388608 | tf_op jit(solution)/shard_map/all_to_all | solution.py:24
  113.9 59.2 %fusion.6 = f32[4,512,1024]{2,1,0:T(8,128)} fusion(f32[512,2048,1]{1,0,2:T(8,128)S(1)} %bitcast.50, f32[2,4,2048,1024]{3,2,1,0:T(8,128)} %param.3), kind=kOutput, calls=%fused_computation.7 | convolution fusion | flops 51539607552 | bytes 46137344 | tf_op jit(solution)/shard_map/sc,pcd->psd/dot_general | solution.py:25
  173.2 0.2 all-gather.5.cloned.1.call-start
  173.4 0.7 constant_dynamic-slice_fusion.1
  174.1 82.9 %reduce-scatter.3.cloned.1.call-done = f32[4,128,1024]{2,1,0:T(8,128)} async-done(((f32[4,512,1024]{2,1,0:T(8,128)}), f32[4,128,1024]{2,1,0:T(8,128)}) %reduce-scatter.3.cloned.1.call-update) | async-done | bytes 2097168 | tf_op jit(solution)/shard_map/reduce_scatter | solution.py:28
  257.0 2.0 multiply_reduce_fusion.2
  259.0 16.2 %psum.14 = f32[4,128]{1,0:T(4,128)S(1)} all-reduce(f32[4,128]{1,0:T(4,128)S(1)} %get-tuple-element.5), channel_id=1, replica_groups=mesh['inb'=4,'outb'=8] {'outb'}, use_global_device_ids=true, to_apply=%region_3.0 | all-reduce | flops 512 | bytes 4096 | tf_op jit(solution)/shard_map/psum | solution.py:30
  275.2 0.9 broadcast_multiply_fusion.1
  276.2 44.2 %all-gather.5.cloned.1.call-done = f32[128,8192]{1,0:T(8,128)} async-done(((f32[128,1024]{1,0:T(8,128)}), f32[128,8192]{1,0:T(8,128)}) %all-gather.5.cloned.1.call-update) | async-done | bytes 4194320 | tf_op jit(solution)/shard_map/all_gather | solution.py:23
  320.4 5.6 %copy.10 = f32[128,8192]{0,1:T(8,128)} copy(f32[128,8192]{1,0:T(8,128)} %all-gather.5.cloned.1.call-done) | data formatting | bytes 8388608 | tf_op jit(solution)/shard_map/all_gather | solution.py:23
  326.0 54.2 %all_to_all.39 = f32[128,4,2048]{0,2,1:T(8,128)} all-to-all(f32[128,4,2048]{0,2,1:T(8,128)} %bitcast.47), channel_id=1, replica_groups=mesh['inb'=4,'outb'=8] {'inb'}, dimensions={1} | all-to-all | bytes 8388608 | tf_op jit(solution)/shard_map/all_to_all | solution.py:24
  380.2 5.4 copy.11
  385.6 59.2 %fusion.9 = f32[4,512,1024]{2,1,0:T(8,128)} fusion(f32[512,2048,1]{1,0,2:T(8,128)} %bitcast.51, f32[2,4,2048,1024]{3,2,1,0:T(8,128)} %param.3), kind=kOutput, calls=%fused_computation.8 | convolution fusion | flops 51539607552 | bytes 46137344 | tf_op jit(solution)/shard_map/sc,pcd->psd/dot_general | solution.py:25
  444.9 83.9 %reduce-scatter.5.cloned.1.call-done = f32[4,128,1024]{2,1,0:T(8,128)} async-done(((f32[4,512,1024]{2,1,0:T(8,128)}), f32[4,128,1024]{2,1,0:T(8,128)}) %reduce-scatter.5.cloned.1.call-update) | async-done | bytes 2097168 | tf_op jit(solution)/shard_map/reduce_scatter | solution.py:28
  528.8 2.0 multiply_reduce_fusion
  530.8 16.2 %psum.15 = f32[4,128]{1,0:T(4,128)S(1)} all-reduce(f32[4,128]{1,0:T(4,128)S(1)} %get-tuple-element.3), channel_id=1, replica_groups=mesh['inb'=4,'outb'=8] {'outb'}, use_global_device_ids=true, to_apply=%region_8.0 | all-reduce | flops 512 | bytes 4096 | tf_op jit(solution)/shard_map/psum | solution.py:30
  547.1 0.5 add_multiply_fusion
  547.6 0.6 pad_maximum_fusion
  548.2 0.9 broadcast_multiply_fusion
  (15 shorter events, 0.2 us)
Async XLA Ops:
  7.2 1.6 copy-start
  7.2 52.6 %all-gather.3.cloned.1.call-start = ((), (), s32[]{:S(2)}) async-start(), calls=%async_computation.4 | async-start | bytes 4718592 | tf_op jit(solution)/shard_map/all_gather | solution.py:23
  9.6 247.4 %reduce-scatter.3.cloned.1.call-start = ((), (), s32[]{:S(2)}) async-start(), calls=%async_computation.5 | async-start | bytes 10485760 | tf_op jit(solution)/shard_map/reduce_scatter | solution.py:28
  173.2 147.2 %all-gather.5.cloned.1.call-start = ((), (), s32[]{:S(2)}) async-start(), calls=%async_computation.6 | async-start | bytes 4718592 | tf_op jit(solution)/shard_map/all_gather | solution.py:23
  276.1 252.7 %reduce-scatter.5.cloned.1.call-start = ((), (), s32[]{:S(2)}) async-start(), calls=%async_computation.7 | async-start | bytes 10485760 | tf_op jit(solution)/shard_map/reduce_scatter | solution.py:28
Sparse Core Ops, SparseCore 0:
  10.2 49.5 all-gather.2
  173.3 83.6 reduce-scatter.2
  276.3 44.0 all-gather.4
  445.0 83.7 reduce-scatter.4
where the time goes:
time: 556 us
  waiting for transfers between devices  261 us (47%)
  blocking collectives  138 us (25%)
  matrix products  118 us (21%)
  local copies, waits for them, and re-layouts  16.5 us (3%)
  between operations  13.8 us (2%)
  other arithmetic  6.98 us (1%)
    reduce_scatter x2, waiting for transfers between devices, on_device(): lax.psum_scatter(partial_terms, 'inb', scatter_dimension=1, tiled=True)  167 us
    dot_general x2, matrix products, on_device(): jnp.einsum('sc,pcd->psd', own_cols, site_cores[site_index], precision=lax...  118 us
    all_to_all x2, blocking collectives, on_device(): lax.all_to_all(sample_rows, 'inb', split_axis=1, concat_axis=0, tiled=True)  106 us
    all_gather x2, waiting for transfers between devices, on_device(): sample_rows = lax.all_gather(current, 'outb', axis=1, tiled=True)  94.3 us
    psum x2, blocking collectives, on_device(): totals = lax.psum(squares, 'outb')  32.4 us
  transfers between devices with their start and end apart: 4, of which 4 were waited for; matrix products, arithmetic and copies ran while one was open for 0% of the time, Pallas kernels for 0%

commit v1 on v0

v1 whole, which is shorter than its diff:
```python
import functools

import jax
import jax.numpy as jnp
from jax import lax
from jax.experimental import pallas as pl
from jax.experimental.pallas import tpu as pltpu
from jax.experimental.layout import Layout, with_layout_constraint
from jax.sharding import PartitionSpec as P

epsilon = 1e-06
MESH = pl.DeviceIdType.MESH
PARTS = 2
SPLIT = 2


def gather_kernel(part, owners, group, x_ref, out_ref, buf, recv, send, first_send, out_sem):
    width = buf.shape[2] // group
    pieces = buf.shape[0]
    me_in, me_out = lax.axis_index("inb"), lax.axis_index("outb")
    place, member = lax.div(me_out, group), lax.rem(me_out, group)
    source = place == me_in
    ahead = jnp.logical_and(place >= me_in, place < owners - 1)
    behind = jnp.logical_and(place <= me_in, place > 0)

    def columns(index):
        return pl.ds(pl.multiple_of(index * width, width), width)

    def sibling(step):
        return lax.rem(member + step, group)

    def hop(piece, slot, out_index):
        where = buf.at[piece, :, columns(member)]
        return pltpu.make_async_remote_copy(
            src_ref=where, dst_ref=where, send_sem=send.at[piece, slot], recv_sem=recv.at[member, piece],
            device_id=(me_in, out_index), device_id_type=MESH,
        )

    def hops(piece, action):
        @pl.when(ahead)
        def _():
            action(hop(piece, 0, me_out + group))

        @pl.when(behind)
        def _():
            action(hop(piece, 1, me_out - group))

        for step in range(1, group):
            action(hop(piece, 1 + step, place * group + sibling(step)))

    def landed(index, piece):
        where = buf.at[piece, :, columns(index)]
        return pltpu.make_async_copy(where, where, recv.at[index, piece])

    def leave(index, piece):
        cols = columns(index)
        return pltpu.make_async_copy(buf.at[piece, :, cols], out_ref.at[piece, :, cols], out_sem.at[index, piece])

    barrier = pltpu.get_barrier_semaphore()

    def greet(in_index, out_index):
        pl.semaphore_signal(barrier, inc=1, device_id=(in_index, out_index), device_id_type=MESH)

    for step in range(1, group):
        greet(me_in, place * group + sibling(step))

    @pl.when(place > me_in)
    def _():
        greet(me_in, me_out - group)

    @pl.when(place < me_in)
    def _():
        greet(me_in, me_out + group)

    if part is None:
        @pl.when(source)
        def _():
            for step in range(1, owners):
                greet(lax.rem(me_in + step, owners), me_out)

    targets = group - 1 + jnp.where(ahead, 1, 0) + jnp.where(behind, 1, 0)
    if part is None:
        targets = targets + jnp.where(source, 0, 1)
    pl.semaphore_wait(barrier, targets)

    def collect(index):
        piece = me_in * SPLIT + index
        return pltpu.make_async_remote_copy(
            src_ref=x_ref.at[index], dst_ref=buf.at[piece, :, columns(member)],
            send_sem=first_send.at[index], recv_sem=recv.at[member, piece],
            device_id=(place, me_out), device_id_type=MESH,
        )

    if part is None:
        @pl.when(source)
        def _():
            for index in range(SPLIT):
                piece = me_in * SPLIT + index
                pltpu.make_async_copy(
                    x_ref.at[index], buf.at[piece, :, columns(member)], recv.at[member, piece]
                ).start()

        @pl.when(jnp.logical_not(source))
        def _():
            for index in range(SPLIT):
                collect(index).start()
    else:
        @pl.when(source)
        def _():
            for piece in range(pieces):
                pltpu.make_async_copy(
                    x_ref.at[piece // SPLIT, part, piece % SPLIT],
                    buf.at[piece, :, columns(member)], recv.at[member, piece],
                ).start()

    for piece in range(pieces):
        landed(member, piece).wait()
        hops(piece, lambda copy: copy.start())
        leave(member, piece).start()
    for piece in range(pieces):
        for step in range(1, group):
            landed(sibling(step), piece).wait()
            leave(sibling(step), piece).start()
    if part is None:
        @pl.when(jnp.logical_not(source))
        def _():
            for index in range(SPLIT):
                collect(index).wait_send()
    for piece in range(pieces):
        hops(piece, lambda copy: copy.wait_send())
        leave(member, piece).wait()
        for step in range(1, group):
            leave(sibling(step), piece).wait()


def gather_rows(x, part, owners, group, rows, width, call_id):
    pieces = owners * SPLIT
    shape = (pieces, rows // SPLIT, group * width)
    sent = pieces * (rows // SPLIT) * width * 4
    out = pl.pallas_call(
        functools.partial(gather_kernel, part, owners, group),
        out_shape=jax.ShapeDtypeStruct(shape, jnp.float32),
        in_specs=[pl.BlockSpec(memory_space=pl.ANY)],
        out_specs=pl.BlockSpec(memory_space=pl.ANY),
        scratch_shapes=[
            pltpu.VMEM(shape, jnp.float32),
            pltpu.SemaphoreType.DMA((group, pieces)),
            pltpu.SemaphoreType.DMA((pieces, 1 + group)),
            pltpu.SemaphoreType.DMA((SPLIT,)),
            pltpu.SemaphoreType.DMA((group, pieces)),
        ],
        compiler_params=pltpu.CompilerParams(collective_id=call_id, has_side_effects=True),
        cost_estimate=pl.CostEstimate(flops=0, bytes_accessed=64 * sent, transcendentals=0),
        name="gather_rows_%d" % call_id,
    )(x)
    return out.reshape(owners * rows, group * width)


def total_kernel(count, x_ref, out_ref, buf, send, recv):
    me_in, me_out = lax.axis_index("inb"), lax.axis_index("outb")
    barrier = pltpu.get_barrier_semaphore()
    for step in range(1, count):
        pl.semaphore_signal(
            barrier, inc=1, device_id=(me_in, lax.rem(me_out + step, count)), device_id_type=MESH
        )
    pl.semaphore_wait(barrier, count - 1)

    def give(step):
        return pltpu.make_async_remote_copy(
            src_ref=x_ref, dst_ref=buf.at[me_out], send_sem=send.at[step], recv_sem=recv.at[me_out],
            device_id=(me_in, lax.rem(me_out + step, count)), device_id_type=MESH,
        )

    for step in range(1, count):
        give(step).start()
    buf[me_out] = x_ref[...]
    for step in range(1, count):
        origin = lax.rem(me_out + step, count)
        pltpu.make_async_copy(x_ref, buf.at[origin], recv.at[origin]).wait()
    total = buf[0]
    for index in range(1, count):
        total = total + buf[index]
    out_ref[...] = total
    for step in range(1, count):
        give(step).wait_send()


def total_over_outb(x, count, call_id):
    height, width = x.shape
    tall, wide = -(-height // 8) * 8, -(-width // 128) * 128
    padded = jnp.pad(x, ((0, tall - height), (0, wide - width)))
    out = pl.pallas_call(
        functools.partial(total_kernel, count),
        out_shape=jax.ShapeDtypeStruct((tall, wide), jnp.float32),
        in_specs=[pl.BlockSpec(memory_space=pltpu.VMEM)],
        out_specs=pl.BlockSpec(memory_space=pltpu.VMEM),
        scratch_shapes=[
            pltpu.VMEM((count, tall, wide), jnp.float32),
            pltpu.SemaphoreType.DMA((count,)),
            pltpu.SemaphoreType.DMA((count,)),
        ],
        compiler_params=pltpu.CompilerParams(collective_id=call_id, has_side_effects=True),
        cost_estimate=pl.CostEstimate(flops=0, bytes_accessed=16_000_000, transcendentals=0),
        name="total_%d" % call_id,
    )(padded)
    return out[:height, :width]


def on_device(owners, outs, site_cores, left_env, outcomes):
    inb_index = lax.axis_index("inb")
    samples_all, width_out = left_env.shape
    sites, outcome_count = site_cores.shape[:2]
    block_rows = samples_all // owners
    rows = block_rows // PARTS
    group = outs // owners
    bond_width = width_out * outs
    levels = jnp.arange(outcome_count, dtype=jnp.int32)
    chosen_ids = lax.dynamic_slice_in_dim(outcomes, inb_index * block_rows, block_rows, 1)
    left_pieces = left_env.reshape(owners, PARTS, SPLIT, rows // SPLIT, width_out)

    log_scale = [jnp.zeros((rows,), jnp.float32)] * PARTS
    current = [left_pieces] * PARTS
    candidates = [None] * PARTS
    probs = [[None] * PARTS for _ in range(sites)]
    row_major = Layout(major_to_minor=(0, 1, 2))
    last = PARTS - 1

    def settle(site_index, part):
        squares = jnp.sum(candidates[part] * candidates[part], axis=2)
        totals = total_over_outb(squares, outs, sites * PARTS + site_index * PARTS + part)
        mean_squares = totals / bond_width + epsilon
        probs[site_index][part] = mean_squares / jnp.sum(mean_squares, axis=0, keepdims=True)
        ids = chosen_ids[site_index, part * rows : (part + 1) * rows]
        onehot = (ids[None, :] == levels[:, None]).astype(jnp.float32)
        chosen = jnp.sum(onehot[:, :, None] * candidates[part], axis=0)
        chosen_mean = jnp.sum(onehot * mean_squares, axis=0)
        log_scale[part] = log_scale[part] + 0.5 * jnp.log(chosen_mean)
        scaled = chosen * lax.rsqrt(chosen_mean)[:, None]
        current[part] = scaled.reshape(SPLIT, rows // SPLIT, width_out)

    for site_index in range(sites):
        for part in range(PARTS):
            if site_index > 0:
                settle(site_index - 1, part)
            own_cols = gather_rows(
                current[part], part if site_index == 0 else None, owners, group, rows, width_out,
                site_index * PARTS + part,
            )
            partial_terms = jnp.einsum(
                "sc,pcd->psd", own_cols, site_cores[site_index], precision=lax.Precision.HIGH
            )
            partial_terms = with_layout_constraint(partial_terms, row_major)
            if part < last:
                waiting = current if site_index == 0 else candidates
                waiting[part + 1], partial_terms = lax.optimization_barrier((waiting[part + 1], partial_terms))
            elif site_index == sites - 1:
                *candidates[:last], partial_terms = lax.optimization_barrier((*candidates[:last], partial_terms))
            summed = lax.psum_scatter(partial_terms, "inb", scatter_dimension=1, tiled=True)
            candidates[part] = with_layout_constraint(summed, row_major)
    for part in range(PARTS):
        settle(sites - 1, part)
    env_out = jnp.concatenate([x.reshape(rows, width_out) for x in current], axis=0)
    prob_stack = jnp.stack([jnp.concatenate(x, axis=1) for x in probs])
    return (env_out, prob_stack, jnp.concatenate(log_scale))


def solution(mesh):
    in_specs = (P(None, None, "inb", "outb"), P(None, "outb"), P())
    out_specs = (P("inb", "outb"), P(None, None, "inb"), P("inb"))
    return jax.shard_map(
        functools.partial(on_device, mesh.shape["inb"], mesh.shape["outb"]),
        mesh=mesh, in_specs=in_specs, out_specs=out_specs, check_vma=False,
    )
```

time: 556 us -> 351 us (0.63)
  waiting for transfers between devices: 261 us -> 68.2 us
  Pallas kernels: 0 us -> 167 us
  blocking collectives: 138 us -> 0 us
  matrix products: 118 us -> 85.3 us
  local copies, waits for them, and re-layouts: 16.5 us -> 4.88 us
    pallas_call x0 -> x8, Pallas kernels: none -> 167 us  [the longest x4 123 us: gather_rows(): pl.pallas_call(functools.partial(gather_kernel, part, owners, group), out...]
    all_to_all x2 -> x0, blocking collectives: 106 us -> none  [on_device(): lax.all_to_all(sample_rows, 'inb', split_axis=1, concat_axis=0, tiled=True)]
    reduce_scatter x2 -> x4, waiting for transfers between devices: 167 us -> 68.1 us  [on_device(): lax.psum_scatter(partial_terms, 'inb', scatter_dimension=1, tiled=True)]
    all_gather x2 -> x0, waiting for transfers between devices: 94.3 us -> none  [on_device(): sample_rows = lax.all_gather(current, 'outb', axis=1, tiled=True)]
    dot_general x2 -> x4, matrix products: 118 us -> 85.3 us  [on_device(): jnp.einsum('sc,pcd->psd', own_cols, site_cores[site_index], precision=lax...]
    psum x2 -> x0, blocking collectives: 32.4 us -> none  [on_device(): totals = lax.psum(squares, 'outb')]
    all_to_all x2 -> x0, local copies, waits for them, and re-layouts: 7.89 us -> none  [on_device(): lax.all_to_all(sample_rows, 'inb', split_axis=1, concat_axis=0, tiled=True)]
    all_gather x1 -> x0, local copies, waits for them, and re-layouts: 5.57 us -> none  [on_device(): sample_rows = lax.all_gather(current, 'outb', axis=1, tiled=True)]
  transfers between devices with their start and end apart: 4 -> 4, of which waited for: 4 -> 4; matrix products, arithmetic and copies ran while one was open for 0% -> 20% of each run, Pallas kernels for 0% -> 38%
where the time goes in v1:
time: 351 us; the launch traced here: 350 us
  Pallas kernels  167 us (48%)
  matrix products  85.3 us (24%)
  waiting for transfers between devices  68.2 us (19%)
  between operations  14 us (4%)
  other arithmetic  11.3 us (3%)
  local copies, waits for them, and re-layouts  4.88 us (1%)
    pallas_call x4, Pallas kernels, gather_rows(): pl.pallas_call(functools.partial(gather_kernel, part, owners, group), out...  123 us
    dot_general x4, matrix products, on_device(): jnp.einsum('sc,pcd->psd', own_cols, site_cores[site_index], precision=lax...  85.3 us
    reduce_scatter x4, waiting for transfers between devices, on_device(): lax.psum_scatter(partial_terms, 'inb', scatter_dimension=1, tiled=True)  68.1 us
    pallas_call x4, Pallas kernels, total_over_outb(): pl.pallas_call(functools.partial(total_kernel, count), out_shape=jax.Shap...  44 us
  transfers between devices with their start and end apart: 4, of which 4 were waited for; matrix products, arithmetic and copies ran while one was open for 20% of the time, Pallas kernels for 38%

profile of v1, /device:TPU:0, one launch (start us, length us, event | category | flops | bytes accessed | tf_op | source)
XLA Modules:
  0.0 350.5 jit_solution(9571450504673493748)
XLA Ops:
  7.2 26.9 %gather_rows_0.1 = f32[8,32,2048]{2,1,0:T(8,128)} custom-call(f32[4,2,2,32,1024]{4,3,2,1,0:T(8,128)} %bitcast.61), custom_call_target="tpu_custom_call" | custom-call | bytes 67108864 | tf_op jit(solution)/shard_map/gather_rows_0/pallas_call | solution.py:140
  34.2 22.5 %fusion.12 = f32[4,256,1024]{2,1,0:T(8,128)} fusion(f32[256,2048,1]{1,0,2:T(8,128)} %bitcast.59, f32[2,4,2048,1024]{3,2,1,0:T(8,128)} %param.3), kind=kOutput, calls=%fused_computation.12 | convolution fusion | flops 12884901888 | bytes 39845888 | tf_op jit(solution)/shard_map/sc,pcd->psd/dot_general | solution.py:249
  56.8 28.8 %gather_rows_1.1 = f32[8,32,2048]{2,1,0:T(8,128)} custom-call(f32[4,2,2,32,1024]{4,3,2,1,0:T(8,128)} %bitcast.62), custom_call_target="tpu_custom_call" | custom-call | bytes 67108864 | tf_op jit(solution)/shard_map/gather_rows_1/pallas_call | solution.py:140
  85.6 21.0 %fusion.15 = f32[4,256,1024]{2,1,0:T(8,128)} fusion(f32[256,2048,1]{1,0,2:T(8,128)} %bitcast.60, f32[2,4,2048,1024]{3,2,1,0:T(8,128)} %param.3), kind=kOutput, calls=%fused_computation.13 | convolution fusion | flops 12884901888 | bytes 39845888 | tf_op jit(solution)/shard_map/sc,pcd->psd/dot_general | solution.py:249
  106.8 14.0 %reduce-scatter.7.cloned.1.call-done = f32[4,64,1024]{2,1,0:T(8,128)} async-done(((f32[4,256,1024]{2,1,0:T(8,128)}), f32[4,64,1024]{2,1,0:T(8,128)}) %reduce-scatter.7.cloned.1.call-update) | async-done | bytes 1048592 | tf_op jit(solution)/shard_map/reduce_scatter | solution.py:258
  120.8 1.4 multiply_reduce_fusion.6
  122.9 7.0 %total_4.1 = f32[8,128]{1,0:T(8,128)} custom-call(f32[8,128]{1,0:T(8,128)} %pad.13.x_ref), custom_call_target="tpu_custom_call" | custom-call | bytes 16000000 | tf_op jit(solution)/shard_map/total_4/pallas_call | solution.py:192
  130.7 0.8 broadcast_multiply_fusion.3.x_ref
  131.5 29.4 %gather_rows_2.1 = f32[8,32,2048]{2,1,0:T(8,128)} custom-call(f32[2,32,1024]{2,1,0:T(8,128)} %broadcast_multiply_fusion.3.x_ref), custom_call_target="tpu_custom_call" | custom-call | bytes 67108864 | tf_op jit(solution)/shard_map/gather_rows_2/pallas_call | solution.py:140
  160.9 20.9 %fusion.18 = f32[4,256,1024]{2,1,0:T(8,128)} fusion(f32[256,2048,1]{1,0,2:T(8,128)} %bitcast.57, f32[2,4,2048,1024]{3,2,1,0:T(8,128)} %param.3), kind=kOutput, calls=%fused_computation.14 | convolution fusion | flops 12884901888 | bytes 39845888 | tf_op jit(solution)/shard_map/sc,pcd->psd/dot_general | solution.py:249
  181.8 5.9 %reduce-scatter.5.cloned.1.call-done = f32[4,64,1024]{2,1,0:T(8,128)} async-done(((f32[4,256,1024]{2,1,0:T(8,128)}), f32[4,64,1024]{2,1,0:T(8,128)}) %reduce-scatter.5.cloned.1.call-update) | async-done | bytes 1048592 | tf_op jit(solution)/shard_map/reduce_scatter | solution.py:258
  187.7 1.1 copy-done.1
  189.7 13.1 %total_5.1 = f32[8,128]{1,0:T(8,128)} custom-call(f32[8,128]{1,0:T(8,128)} %pad.14.x_ref), custom_call_target="tpu_custom_call" | custom-call | bytes 16000000 | tf_op jit(solution)/shard_map/total_5/pallas_call | solution.py:192
  203.5 0.8 broadcast_multiply_fusion.2.x_ref
  204.3 37.5 %gather_rows_3.1 = f32[8,32,2048]{2,1,0:T(8,128)} custom-call(f32[2,32,1024]{2,1,0:T(8,128)} %broadcast_multiply_fusion.2.x_ref), custom_call_target="tpu_custom_call" | custom-call | bytes 67108864 | tf_op jit(solution)/shard_map/gather_rows_3/pallas_call | solution.py:140
  241.8 20.9 %fusion.21 = f32[4,256,1024]{2,1,0:T(8,128)} fusion(f32[256,2048,1]{1,0,2:T(8,128)} %bitcast.58, f32[2,4,2048,1024]{3,2,1,0:T(8,128)} %param.3), kind=kOutput, calls=%fused_computation.15 | convolution fusion | flops 12884901888 | bytes 39845888 | tf_op jit(solution)/shard_map/sc,pcd->psd/dot_general | solution.py:249
  262.7 0.8 reduce-scatter.9.cloned.1.call-done
  263.6 1.1 copy-done.2
  265.5 16.8 %total_6.1 = f32[8,128]{1,0:T(8,128)} custom-call(f32[8,128]{1,0:T(8,128)} %pad.15.x_ref), custom_call_target="tpu_custom_call" | custom-call | bytes 16000000 | tf_op jit(solution)/shard_map/total_6/pallas_call | solution.py:192
  283.8 47.4 %reduce-scatter.11.cloned.1.call-done = f32[4,64,1024]{2,1,0:T(8,128)} async-done(((f32[4,256,1024]{2,1,0:T(8,128)}), f32[4,64,1024]{2,1,0:T(8,128)}) %reduce-scatter.11.cloned.1.call-update) | async-done | bytes 1048592 | tf_op jit(solution)/shard_map/reduce_scatter | solution.py:258
  331.2 1.4 multiply_reduce_fusion
  333.3 7.1 %total_7.1 = f32[8,128]{1,0:T(8,128)} custom-call(f32[8,128]{1,0:T(8,128)} %pad.16.x_ref), custom_call_target="tpu_custom_call" | custom-call | bytes 16000000 | tf_op jit(solution)/shard_map/total_7/pallas_call | solution.py:192
  340.3 0.7 fusion.31
  341.8 0.8 pad_maximum_fusion
  (46 shorter events, 8.3 us)
Async XLA Ops:
  7.2 99.5 %copy-start = (s32[2,512]{1,0:T(2,128)S(1)}, s32[2,512]{1,0:T(2,128)}, u32[]{:S(2)}) copy-start(s32[2,512]{1,0:T(2,128)} %param.5) | copy-start | bytes 12292
  7.2 113.7 %reduce-scatter.7.cloned.1.call-start = ((), (), s32[]{:S(2)}) async-start(), calls=%async_computation.5 | async-start | bytes 5242880 | tf_op jit(solution)/shard_map/reduce_scatter | solution.py:258
  56.7 130.9 %reduce-scatter.5.cloned.1.call-start = ((), (), s32[]{:S(2)}) async-start(), calls=%async_computation.4 | async-start | bytes 5242880 | tf_op jit(solution)/shard_map/reduce_scatter | solution.py:258
  106.6 156.8 %reduce-scatter.9.cloned.1.call-start = ((), (), s32[]{:S(2)}) async-start(), calls=%async_computation.6 | async-start | bytes 5242880 | tf_op jit(solution)/shard_map/reduce_scatter | solution.py:258
  187.6 1.2 copy-start.1
  187.7 143.6 %reduce-scatter.11.cloned.1.call-start = ((), (), s32[]{:S(2)}) async-start(), calls=%async_computation.7 | async-start | bytes 5242880 | tf_op jit(solution)/shard_map/reduce_scatter | solution.py:258
  262.7 0.8 copy-start.4
  262.7 0.9 copy-start.3
  263.5 1.2 copy-start.2
Sparse Core Ops, SparseCore 0:
  56.8 63.9 reduce-scatter.6
  123.8 63.7 reduce-scatter.4
  190.6 72.8 reduce-scatter.8
  266.3 64.8 reduce-scatter.10
